TPU v7x, 512 devices: a whole 4x4x16 slice. The times are simulated.
512 devices in a mesh: dp: 32 (over y, x, core), seq: 16 (over z).
Axes of the slice: x: 4, y: 4, z: 16, core: 2. Of those that a mesh axis runs over, the one named last changes fastest.
Arguments:
- queries: bfloat16 [32, 2048, 2048], P('dp', 'seq')
- keys: bfloat16 [32, 2048, 2048], P('dp', 'seq')
- events: bfloat16 [32, 2048, 2048], P('dp', 'seq'), may hold values from -6 to 6
- out_grad: bfloat16 [32, 2048, 2048], P('dp', 'seq'), may hold values from -6 to 6
- segment_ids: int32 [32, 2048], P('dp', 'seq'), may hold values from 0 to 63, never falling along the last dimension, each value on 1 to 512 neighbouring positions
- block_list: int32 [32, 16, 4], P('dp'), may hold values from 0 to 15, as said below
- conv_weight: float32 [64, 2048], replicated, may hold values from -0.75 to 0.75
Outputs:
- query_grad: bfloat16 [32, 2048, 2048], P('dp', 'seq')
- key_grad: bfloat16 [32, 2048, 2048], P('dp', 'seq')
- event_grad: bfloat16 [32, 2048, 2048], P('dp', 'seq')
- filter_grad: float32 [64, 2048], replicated
Inputs may be any that keep to these rules, and one draw needn't show every extreme that they name: `block_list`: entry 0 for query block b is b itself; every entry for block b lies in 0 .. b; entries may repeat.
All inputs are finite; a program needn't handle non-finite values.
Results may differ from a plain program's by a relative error of at most 0.015.
Values may be sent and summed in bfloat16 or wider, within the bound.
A program may use at most 64 MiB of HBM per device.

v0:
```python
import jax
import jax.numpy as jnp
from jax import lax
from jax.sharding import PartitionSpec as P

HD = 64
BLOCK = 128


def shifted(value, axis, steps):
    count = lax.axis_size(axis)
    initial, last = (max(0, -steps), min(count, count - steps))
    return lax.ppermute(value, axis, [(source, source + steps) for source in range(initial, last)])


def contract(form, left, right, exact):
    if exact:
        return jnp.einsum(
            form, left, right, precision=lax.Precision.HIGHEST, preferred_element_type=jnp.float32
        )
    return jnp.einsum(form, left, right, preferred_element_type=jnp.float32)


def causal_conv(padded, ids_ext, weight, count):
    taps = weight.shape[0]
    own = ids_ext[taps - 1 : taps - 1 + count]
    total = jnp.zeros((count, padded.shape[1]), jnp.float32)
    for step in range(taps):
        begin = taps - 1 - step
        piece = padded[begin : begin + count].astype(jnp.float32)
        match = (ids_ext[begin : begin + count] == own)[:, None]
        total = total + jnp.where(match, piece * weight[step : step + 1], 0.0)
    return total


def anti_conv(padded, ids_ext, weight, count):
    taps = weight.shape[0]
    own = ids_ext[0:count]
    total = jnp.zeros((count, padded.shape[1]), jnp.float32)
    for step in range(taps):
        piece = padded[step : step + count].astype(jnp.float32)
        match = (ids_ext[step : step + count] == own)[:, None]
        total = total + jnp.where(match, piece * weight[step : step + 1], 0.0)
    return total


def tap_gradient(grad, padded, ids_ext, taps):
    count = grad.shape[0]
    own = ids_ext[taps - 1 : taps - 1 + count]
    grad_wide = grad.astype(jnp.float32)
    sums = []
    for step in range(taps):
        begin = taps - 1 - step
        piece = padded[begin : begin + count].astype(jnp.float32)
        match = (ids_ext[begin : begin + count] == own)[:, None]
        sums.append(jnp.sum(jnp.where(match, piece * grad_wide, 0.0), axis=0))
    return jnp.stack(sums, axis=0)


def block_attention(query, key_rows, value, grad, ids, blist, block):
    tokens, head_dim = query.shape
    nblk = tokens // block
    nsel = blist.shape[1]
    scale = head_dim ** (-0.5)
    same = blist[:, :, None] == blist[:, None, :]
    before = jnp.arange(nsel)[None, :, None] > jnp.arange(nsel)[None, None, :]
    fresh = jnp.logical_not(jnp.any(same & before, axis=2))
    chosen = (blist[:, :, None] == jnp.arange(nblk, dtype=jnp.int32)[None, None, :]) & fresh[
        :, :, None
    ]
    picker = chosen.astype(jnp.bfloat16)
    q_blk = query.reshape(nblk, block, head_dim)
    k_blk = key_rows.reshape(nblk, block, head_dim)
    v_blk = value.reshape(nblk, block, head_dim)
    g_blk = grad.reshape(nblk, block, head_dim)
    k_sel = contract("bjc,cmd->bjmd", picker, k_blk, False).astype(jnp.bfloat16)
    v_sel = contract("bjc,cmd->bjmd", picker, v_blk, False).astype(jnp.bfloat16)
    id_blk = ids.reshape(nblk, block)
    id_sel = jnp.sum(jnp.where(chosen[:, :, :, None], id_blk[None, None, :, :], 0), axis=2)
    q_pos = (
        jnp.arange(nblk, dtype=jnp.int32)[:, None] * block
        + jnp.arange(block, dtype=jnp.int32)[None, :]
    )
    k_pos = blist[:, :, None] * block + jnp.arange(block, dtype=jnp.int32)[None, None, :]
    allowed = (
        fresh[:, None, :, None]
        & (k_pos[:, None] <= q_pos[:, :, None, None])
        & (id_sel[:, None] == id_blk[:, :, None, None])
    )
    scores = contract("bid,bjmd->bijm", q_blk, k_sel, False) * scale
    scores = jnp.where(allowed, scores, -1e30)
    top = jnp.max(scores, axis=(2, 3), keepdims=True)
    weights = jnp.where(allowed, jnp.exp(scores - top), 0.0)
    probs = weights / jnp.sum(weights, axis=(2, 3), keepdims=True)
    probs_low = probs.astype(jnp.bfloat16)
    attended = contract("bijm,bjmd->bid", probs_low, v_sel, False)
    delta = jnp.sum(g_blk.astype(jnp.float32) * attended, axis=2)
    dprobs = contract("bid,bjmd->bijm", g_blk, v_sel, False)
    dscores = (probs * (dprobs - delta[:, :, None, None])).astype(jnp.bfloat16)
    q_grad = (contract("bijm,bjmd->bid", dscores, k_sel, False) * scale).astype(jnp.bfloat16)
    k_slot = contract("bijm,bid->bjmd", dscores, q_blk, False) * scale
    v_slot = contract("bijm,bid->bjmd", probs_low, g_blk, False)
    spread = chosen.astype(jnp.float32)
    k_grad = contract("bjc,bjmd->cmd", spread, k_slot, True).astype(jnp.bfloat16)
    v_grad = contract("bjc,bjmd->cmd", spread, v_slot, True).astype(jnp.bfloat16)
    return (
        q_grad.reshape(tokens, head_dim),
        k_grad.reshape(tokens, head_dim),
        v_grad.reshape(tokens, head_dim),
    )


def heads_attention(query, key_rows, value, grad, ids, blist, head_dim, block):
    tokens, width = query.shape
    heads = width // head_dim

    def split(array):
        return array.reshape(tokens, heads, head_dim).transpose(1, 0, 2)

    def join(array):
        return array.transpose(1, 0, 2).reshape(tokens, width)

    def one_head(item):
        return block_attention(item[0], item[1], item[2], item[3], ids, blist, block)

    q_grad, k_grad, v_grad = lax.map(
        one_head, (split(query), split(key_rows), split(value), split(grad))
    )
    return (join(q_grad), join(k_grad), join(v_grad))


def per_device(queries, keys, events, out_grad, segment_ids, block_list, conv_weight):
    query = queries[0]
    key_rows = keys[0]
    feats = events[0]
    grad = out_grad[0]
    blist = block_list[0]
    rows, width = query.shape
    taps = conv_weight.shape[0]
    shards = lax.axis_size("dp") * lax.axis_size("seq")
    position = lax.axis_index("seq")
    all_ids = lax.all_gather(segment_ids, "seq", axis=1, tiled=True)[0]
    rim = jnp.zeros((taps - 1,), jnp.int32)
    ids_all = jnp.concatenate([rim, all_ids + 1, rim])
    left_ids = lax.dynamic_slice_in_dim(ids_all, position * rows, rows + taps - 1, 0)
    right_ids = lax.dynamic_slice_in_dim(ids_all, position * rows + taps - 1, rows + taps - 1, 0)
    earlier = shifted(feats[rows - (taps - 1) :], "seq", 1)
    padded = jnp.concatenate([earlier, feats], axis=0)
    values = causal_conv(padded, left_ids, conv_weight, rows).astype(jnp.bfloat16)
    head_q, head_k, head_v, head_g = (
        lax.all_to_all(query, "seq", split_axis=1, concat_axis=0, tiled=True),
        lax.all_to_all(key_rows, "seq", split_axis=1, concat_axis=0, tiled=True),
        lax.all_to_all(values, "seq", split_axis=1, concat_axis=0, tiled=True),
        lax.all_to_all(grad, "seq", split_axis=1, concat_axis=0, tiled=True),
    )
    q_grad, k_grad, v_grad = heads_attention(
        head_q, head_k, head_v, head_g, all_ids, blist, HD, BLOCK
    )
    q_back, k_back, v_back = (
        lax.all_to_all(q_grad, "seq", split_axis=0, concat_axis=1, tiled=True),
        lax.all_to_all(k_grad, "seq", split_axis=0, concat_axis=1, tiled=True),
        lax.all_to_all(v_grad, "seq", split_axis=0, concat_axis=1, tiled=True),
    )
    later = shifted(v_back[: taps - 1], "seq", -1)
    after = jnp.concatenate([v_back, later], axis=0)
    e_grad = anti_conv(after, right_ids, conv_weight, rows).astype(jnp.bfloat16)
    f_local = tap_gradient(v_back, padded, left_ids, taps)
    f_grad = lax.psum(f_local, ("dp", "seq")) / shards
    return (q_back[None], k_back[None], e_grad[None], f_grad)


def solution(mesh):
    in_specs = (
        P("dp", "seq", None),
        P("dp", "seq", None),
        P("dp", "seq", None),
        P("dp", "seq", None),
        P("dp", "seq"),
        P("dp", None, None),
        P(),
    )
    out_specs = (P("dp", "seq", None), P("dp", "seq", None), P("dp", "seq", None), P())
    return jax.shard_map(
        per_device, mesh=mesh, in_specs=in_specs, out_specs=out_specs, check_vma=False
    )
```

profile of v0, /device:TPU:4, one launch (start us, length us, event | category | flops | bytes accessed | tf_op | source)
XLA Modules:
  0.0 903.5 jit_solution(13056101979047803530)
XLA Ops:
  9.3 15.2 %all-to-all-start = ((bf16[128,16,128]{0,2,1:T(8,128)(2,1)}), bf16[128,16,128]{0,2,1:T(8,128)(2,1)S(1)}, u32[]{:S(2)}, u32[]{:S(2)}) async-start(bf16[128,16,128]{0,2,1:T(8,128)(2,1)} %bitcast.18), calls=%async_computation | async-start | bytes 1048576 | tf_op jit(solution)/shard_map/all_to_all | solution.py:151
  31.7 52.5 %all_gather.3 = s32[1,2048]{1,0:T(1,128)S(1)} all-gather(s32[1,128]{1,0:T(1,128)S(1)} %copy-done.122), channel_id=1, replica_groups=mesh['dp'=32,'seq'=16] {'seq'}, dimensions={1}, use_global_device_ids=true | all-gather | bytes 8704 | tf_op jit(solution)/shard_map/all_gather | solution.py:142
  87.2 8.8 all-to-all-start.1
  101.4 16.4 %all-to-all-done.1 = bf16[128,16,128]{0,2,1:T(8,128)(2,1)S(1)} async-done(((bf16[128,16,128]{0,2,1:T(8,128)(2,1)}), bf16[128,16,128]{0,2,1:T(8,128)(2,1)S(1)}, u32[]{:S(2)}, u32[]{:S(2)}) %all-to-all-start.1) | async-done | bytes 524320 | tf_op jit(solution)/shard_map/all_to_all | solution.py:152
  117.8 7.0 all-to-all-start.2
  124.9 40.2 %fusion.322 = bf16[128,2048]{0,1:T(8,128)(2,1)S(1)} fusion(bf16[128,2048]{0,1:T(8,128)(2,1)S(1)} %bitcast.375, f32[2048]{0:T(1024)S(1)} %bitcast.429, f32[2048]{0:T(1024)S(1)} %bitcast.431, f32[2048]{0:T(1024)S(1)} %bitcast.435, f32[2048]{0:T(1024)S(1)} %bitcast.437, f32[2048]{0:T(1024)S(1)} %bitcast.439, f32[2048]{0:T(1024)S(1)} %bitcast.441, ...), kind=kLoop, calls=%fused_computation.710 | loop fusion | flops 116391936 | bytes 1838976 | tf_op jit(solution)/shard_map/convert_element_type | solution.py:149
  166.1 12.0 %all-to-all-start.3 = ((bf16[128,16,128]{2,0,1:T(8,128)(2,1)}), bf16[128,16,128]{2,0,1:T(8,128)(2,1)S(1)}, u32[]{:S(2)}, u32[]{:S(2)}) async-start(bf16[128,16,128]{2,0,1:T(8,128)(2,1)} %copy.195), calls=%async_computation.3 | async-start | bytes 1048576 | tf_op jit(solution)/shard_map/all_to_all | solution.py:153
  185.8 17.3 %all-to-all-done.3 = bf16[128,16,128]{2,0,1:T(8,128)(2,1)S(1)} async-done(((bf16[128,16,128]{2,0,1:T(8,128)(2,1)}), bf16[128,16,128]{2,0,1:T(8,128)(2,1)S(1)}, u32[]{:S(2)}, u32[]{:S(2)}) %all-to-all-start.3) | async-done | bytes 524320 | tf_op jit(solution)/shard_map/all_to_all | solution.py:153
  204.6 67.1 %while.18 = (s32[]{:T(128)}, bf16[2,2048,64]{1,2,0:T(8,128)(2,1)}, bf16[2,2048,64]{1,2,0:T(8,128)(2,1)}, bf16[2,2048,64]{1,2,0:T(8,128)(2,1)}, pred[16,4]{1,0:T(...) while((s32[]{:T(128)}, bf16[2,2048,64]{1,2,0:T(8,128)(2,1)}, ...), condition=%wide.region_6.7_spmd, body=%wide.region_1.6_spmd.sunk | while | flops 1074403328 | bytes 83230208 | solution.py:126
  207.2 4.9 fusion.503
  240.7 4.9 fusion.503
  273.9 6.5 all-to-all-start.4
  282.8 24.3 %all-to-all-done.4 = bf16[16,128,128]{1,2,0:T(8,128)(2,1)S(1)} async-done(((bf16[16,128,128]{1,2,0:T(8,128)(2,1)}), bf16[16,128,128]{1,2,0:T(8,128)(2,1)S(1)}, u32[]{:S(2)}, u32[]{:S(2)}) %all-to-all-start.4) | async-done | bytes 524320 | tf_op jit(solution)/shard_map/all_to_all | solution.py:160
  307.1 16.3 %all-to-all-start.5 = ((bf16[16,128,128]{2,1,0:T(8,128)(2,1)}), bf16[16,128,128]{2,1,0:T(8,128)(2,1)S(1)}, u32[]{:S(2)}, u32[]{:S(2)}) async-start(bf16[16,128,128]{2,1,0:T(8,128)(2,1)} %copy.199), calls=%async_computation.5 | async-start | bytes 1048576 | tf_op jit(solution)/shard_map/all_to_all | solution.py:161
  324.8 25.9 %all-to-all-done.5 = bf16[16,128,128]{2,1,0:T(8,128)(2,1)S(1)} async-done(((bf16[16,128,128]{2,1,0:T(8,128)(2,1)}), bf16[16,128,128]{2,1,0:T(8,128)(2,1)S(1)}, u32[]{:S(2)}, u32[]{:S(2)}) %all-to-all-start.5) | async-done | bytes 524320 | tf_op jit(solution)/shard_map/all_to_all | solution.py:161
  350.7 7.0 all-to-all-start.6
  360.8 25.3 %all-to-all-done.6 = bf16[16,128,128]{2,1,0:T(8,128)(2,1)S(1)} async-done(((bf16[16,128,128]{2,1,0:T(8,128)(2,1)}), bf16[16,128,128]{2,1,0:T(8,128)(2,1)S(1)}, u32[]{:S(2)}, u32[]{:S(2)}) %all-to-all-start.6) | async-done | bytes 524320 | tf_op jit(solution)/shard_map/all_to_all | solution.py:162
  395.0 4.1 fusion.235
  414.2 4.2 fusion.295
  418.5 4.3 fusion.307
  422.7 4.2 fusion.319
  429.7 5.8 stack.259
  435.9 41.2 %fusion.447 = bf16[1,128,2048]{1,2,0:T(8,128)(2,1)S(1)} fusion(f32[2048]{0:T(1024)S(1)} %bitcast.430, bf16[63,2048]{0,1:T(8,128)(2,1)S(1)} %collective-permute-done.1, bf16[128,2048]{0,1:T(8,128)(2,1)S(1)} %bitcast.391, pred[128]{0:T(512)(128)(4,1)S(1)} %get-tuple-element.460, f32[2048]{0:T(1024)S(1)} %bitcast.432, ...), kind=kLoop, calls=%fused_computation.838 | loop fusion | flops 116391936 | bytes 1838976 | tf_op jit(solution)/shard_map/broadcast_in_dim | solution.py:169
  478.1 416.2 %all-reduce.2.cloned.1.call-done = f32[64,2048]{1,0:T(8,128)} async-done(((f32[64,2048]{1,0:T(8,128)}), f32[64,2048]{1,0:T(8,128)}) %all-reduce.2.cloned.1.call-update) | async-done | bytes 524304 | tf_op jit(solution)/shard_map/psum | solution.py:168
  (390 shorter events, 121.5 us)
Async XLA Ops:
  9.3 77.8 %all-to-all-start = ((bf16[128,16,128]{0,2,1:T(8,128)(2,1)}), bf16[128,16,128]{0,2,1:T(8,128)(2,1)S(1)}, u32[]{:S(2)}, u32[]{:S(2)}) async-start(bf16[128,16,128]{0,2,1:T(8,128)(2,1)} %bitcast.18), calls=%async_computation | async-start | bytes 1048576 | tf_op jit(solution)/shard_map/all_to_all | solution.py:151
  26.8 98.0 %collective-permute-start = (bf16[63,2048]{0,1:T(8,128)(2,1)}, bf16[63,2048]{0,1:T(8,128)(2,1)S(1)}, u32[]{:S(2)}, u32[]{:S(2)}) collective-permute-start(bf16[63,2048]{0,1:T(8,128)(2,1)} %slice_bitcast_fusion), channel_id=1, source_target_pairs={{0,1},{1,2},{2,3},{3,4},{4,5},{5,6},{6,7},{7,8},{8,9},{9,10},{10,1... | collective-permute-start | bytes 774152 | tf_op jit(solution)/shard_map/ppermute | solution.py:13
  87.2 91.0 %copy-start.2 = (s32[1,16,4]{1,2,0:T(4,128)S(1)}, s32[1,16,4]{1,2,0:T(4,128)}, u32[]{:S(2)}) copy-start(s32[1,16,4]{1,2,0:T(4,128)} %param.14) | copy-start | bytes 772
  87.2 30.6 %all-to-all-start.1 = ((bf16[128,16,128]{0,2,1:T(8,128)(2,1)}), bf16[128,16,128]{0,2,1:T(8,128)(2,1)S(1)}, u32[]{:S(2)}, u32[]{:S(2)}) async-start(bf16[128,16,128]{0,2,1:T(8,128)(2,1)} %bitcast.21), calls=%async_computation.1 | async-start | bytes 1048576 | tf_op jit(solution)/shard_map/all_to_all | solution.py:152
  97.1 85.8 %copy-start.30 = (f32[1,2048]{1,0:T(1,128)}, f32[1,2048]{1,0:T(1,128)S(1)}, u32[]{:S(2)}) copy-start(f32[1,2048]{1,0:T(1,128)S(1)} %get-tuple-element.351) | copy-start | bytes 24580
  97.1 85.8 %copy-start.32 = (f32[1,2048]{1,0:T(1,128)}, f32[1,2048]{1,0:T(1,128)S(1)}, u32[]{:S(2)}) copy-start(f32[1,2048]{1,0:T(1,128)S(1)} %get-tuple-element.352) | copy-start | bytes 24580
  97.1 85.8 %copy-start.34 = (f32[1,2048]{1,0:T(1,128)}, f32[1,2048]{1,0:T(1,128)S(1)}, u32[]{:S(2)}) copy-start(f32[1,2048]{1,0:T(1,128)S(1)} %get-tuple-element.353) | copy-start | bytes 24580
  97.1 85.8 %copy-start.36 = (f32[1,2048]{1,0:T(1,128)}, f32[1,2048]{1,0:T(1,128)S(1)}, u32[]{:S(2)}) copy-start(f32[1,2048]{1,0:T(1,128)S(1)} %get-tuple-element.354) | copy-start | bytes 24580
  97.1 85.8 %copy-start.38 = (f32[1,2048]{1,0:T(1,128)}, f32[1,2048]{1,0:T(1,128)S(1)}, u32[]{:S(2)}) copy-start(f32[1,2048]{1,0:T(1,128)S(1)} %get-tuple-element.355) | copy-start | bytes 24580
  97.1 85.8 %copy-start.40 = (f32[1,2048]{1,0:T(1,128)}, f32[1,2048]{1,0:T(1,128)S(1)}, u32[]{:S(2)}) copy-start(f32[1,2048]{1,0:T(1,128)S(1)} %get-tuple-element.356) | copy-start | bytes 24580
  97.1 85.8 %copy-start.42 = (f32[1,2048]{1,0:T(1,128)}, f32[1,2048]{1,0:T(1,128)S(1)}, u32[]{:S(2)}) copy-start(f32[1,2048]{1,0:T(1,128)S(1)} %get-tuple-element.357) | copy-start | bytes 24580
  117.8 48.3 %all-to-all-start.2 = ((bf16[128,16,128]{0,2,1:T(8,128)(2,1)}), bf16[128,16,128]{0,2,1:T(8,128)(2,1)S(1)}, u32[]{:S(2)}, u32[]{:S(2)}) async-start(bf16[128,16,128]{0,2,1:T(8,128)(2,1)} %bitcast.24), calls=%async_computation.2 | async-start | bytes 1048576 | tf_op jit(solution)/shard_map/all_to_all | solution.py:154
  166.1 37.0 %all-to-all-start.3 = ((bf16[128,16,128]{2,0,1:T(8,128)(2,1)}), bf16[128,16,128]{2,0,1:T(8,128)(2,1)S(1)}, u32[]{:S(2)}, u32[]{:S(2)}) async-start(bf16[128,16,128]{2,0,1:T(8,128)(2,1)} %copy.195), calls=%async_computation.3 | async-start | bytes 1048576 | tf_op jit(solution)/shard_map/all_to_all | solution.py:153
  273.9 33.2 %all-to-all-start.4 = ((bf16[16,128,128]{1,2,0:T(8,128)(2,1)}), bf16[16,128,128]{1,2,0:T(8,128)(2,1)S(1)}, u32[]{:S(2)}, u32[]{:S(2)}) async-start(bf16[16,128,128]{1,2,0:T(8,128)(2,1)} %copy.198), calls=%async_computation.4 | async-start | bytes 1048576 | tf_op jit(solution)/shard_map/all_to_all | solution.py:160
  282.8 105.0 %copy-start.99 = (pred[128]{0:T(512)(128)(4,1)S(1)}, pred[128]{0:T(512)(128)(4,1)}, u32[]{:S(2)}) copy-start(pred[128]{0:T(512)(128)(4,1)} %get-tuple-element.523) | copy-start | bytes 388
  282.8 105.0 %copy-start.102 = (pred[128]{0:T(512)(128)(4,1)S(1)}, pred[128]{0:T(512)(128)(4,1)}, u32[]{:S(2)}) copy-start(pred[128]{0:T(512)(128)(4,1)} %get-tuple-element.461) | copy-start | bytes 388
  282.8 105.0 %copy-start.103 = (pred[128]{0:T(512)(128)(4,1)S(1)}, pred[128]{0:T(512)(128)(4,1)}, u32[]{:S(2)}) copy-start(pred[128]{0:T(512)(128)(4,1)} %get-tuple-element.470) | copy-start | bytes 388
  282.8 105.0 %copy-start.104 = (pred[128]{0:T(512)(128)(4,1)S(1)}, pred[128]{0:T(512)(128)(4,1)}, u32[]{:S(2)}) copy-start(pred[128]{0:T(512)(128)(4,1)} %get-tuple-element.479) | copy-start | bytes 388
  282.8 105.0 %copy-start.105 = (pred[128]{0:T(512)(128)(4,1)S(1)}, pred[128]{0:T(512)(128)(4,1)}, u32[]{:S(2)}) copy-start(pred[128]{0:T(512)(128)(4,1)} %get-tuple-element.488) | copy-start | bytes 388
  282.8 105.0 %copy-start.121 = (pred[128]{0:T(512)(128)(4,1)S(1)}, pred[128]{0:T(512)(128)(4,1)}, u32[]{:S(2)}) copy-start(pred[128]{0:T(512)(128)(4,1)} %get-tuple-element.497) | copy-start | bytes 388
  307.1 43.6 %all-to-all-start.5 = ((bf16[16,128,128]{2,1,0:T(8,128)(2,1)}), bf16[16,128,128]{2,1,0:T(8,128)(2,1)S(1)}, u32[]{:S(2)}, u32[]{:S(2)}) async-start(bf16[16,128,128]{2,1,0:T(8,128)(2,1)} %copy.199), calls=%async_computation.5 | async-start | bytes 1048576 | tf_op jit(solution)/shard_map/all_to_all | solution.py:161
  350.7 35.4 %all-to-all-start.6 = ((bf16[16,128,128]{2,1,0:T(8,128)(2,1)}), bf16[16,128,128]{2,1,0:T(8,128)(2,1)S(1)}, u32[]{:S(2)}, u32[]{:S(2)}) async-start(bf16[16,128,128]{2,1,0:T(8,128)(2,1)} %copy.201), calls=%async_computation.6 | async-start | bytes 1048576 | tf_op jit(solution)/shard_map/all_to_all | solution.py:162
  357.7 536.6 %all-reduce.2.cloned.1.call-start = ((), (), s32[]{:S(2)}) async-start(), calls=%async_computation.7 | async-start | bytes 1048576 | tf_op jit(solution)/shard_map/psum | solution.py:168
  386.4 49.1 %collective-permute-start.1 = (bf16[63,2048]{0,1:T(8,128)(2,1)S(1)}, bf16[63,2048]{0,1:T(8,128)(2,1)S(1)}, u32[]{:S(2)}, u32[]{:S(2)}) collective-permute-start(bf16[63,2048]{0,1:T(8,128)(2,1)S(1)} %bitcast.390), channel_id=1, source_target_pairs={{1,0},{2,1},{3,2},{4,3},{5,4},{6,5},{7,6},{8,7},{9,8},{10,9},{11,1... | collective-permute-start | bytes 774152 | tf_op jit(solution)/shard_map/ppermute | solution.py:13
  (113 other events, 4765.0 us)
Sparse Core Ops, SparseCore 0:
  435.6 458.6 all-reduce.1
where the time goes:
time: 913 us; the launch traced here: 903 us
  waiting for transfers between devices  525 us (58%)
  other arithmetic  143 us (16%)
  starting transfers between devices  78.1 us (9%)
  blocking collectives  52.5 us (6%)
  local copies, waits for them, and re-layouts  51.7 us (6%)
  matrix products  35.5 us (4%)
  between operations  16.6 us (2%)
    psum x1, waiting for transfers between devices, per_device(): f_grad = lax.psum(f_local, ('dp', 'seq')) / shards  416 us
    all_gather x1, blocking collectives, per_device(): all_ids = lax.all_gather(segment_ids, 'seq', axis=1, tiled=True)[0]  52.5 us
    broadcast_in_dim x1, other arithmetic, per_device(): return (q_back[None], k_back[None], e_grad[None], f_grad)  41.2 us
    reduce_sum x11, other arithmetic, tap_gradient(): sums.append(jnp.sum(jnp.where(match, piece * grad_wide, 0.0), axis=0))  41 us
    convert_element_type x1, other arithmetic, per_device(): causal_conv(padded, left_ids, conv_weight, rows).astype(jnp.bfloat16)  40.2 us
    dot_general x16, matrix products, contract(): return jnp.einsum(form, left, right, preferred_element_type=jnp.float32)  26.3 us
    all_to_all x1, waiting for transfers between devices, per_device(): lax.all_to_all(k_grad, 'seq', split_axis=0, concat_axis=1, tiled=True)  25.9 us
    all_to_all x1, waiting for transfers between devices, per_device(): lax.all_to_all(v_grad, 'seq', split_axis=0, concat_axis=1, tiled=True)  25.3 us
  transfers between devices with their start and end apart: 10, of which 6 were waited for; matrix products, arithmetic and copies ran while one was open for 17% of the time, Pallas kernels for 0%

commit v1 on v0

--- a/solution.py
+++ b/solution.py
@@ -165,7 +165,7 @@
     after = jnp.concatenate([v_back, later], axis=0)
     e_grad = anti_conv(after, right_ids, conv_weight, rows).astype(jnp.bfloat16)
     f_local = tap_gradient(v_back, padded, left_ids, taps)
-    f_grad = lax.psum(f_local, ("dp", "seq")) / shards
+    f_grad = lax.psum(lax.psum(f_local, "seq"), "dp") / shards
     return (q_back[None], k_back[None], e_grad[None], f_grad)
 
 

time: 913 us -> 666 us (0.73)
  the two profiles are of different devices: /device:TPU:4 before, /device:TPU:1 now
where the time goes in v1:
time: 666 us; the launch traced here: 656 us
  waiting for transfers between devices  273 us (41%)
  other arithmetic  141 us (21%)
  starting transfers between devices  93.1 us (14%)
  local copies, waits for them, and re-layouts  50.1 us (8%)
  blocking collectives  46.4 us (7%)
  matrix products  35.5 us (5%)
  between operations  16.5 us (2%)
    psum x2, waiting for transfers between devices, per_device(): f_grad = lax.psum(lax.psum(f_local, 'seq'), 'dp') / shards  230 us
    all_gather x1, blocking collectives, per_device(): all_ids = lax.all_gather(segment_ids, 'seq', axis=1, tiled=True)[0]  46.4 us
    convert_element_type x1, other arithmetic, per_device(): causal_conv(padded, left_ids, conv_weight, rows).astype(jnp.bfloat16)  40.2 us
    reduce_sum x11, other arithmetic, tap_gradient(): sums.append(jnp.sum(jnp.where(match, piece * grad_wide, 0.0), axis=0))  39.9 us
    broadcast_in_dim x1, other arithmetic, per_device(): return (q_back[None], k_back[None], e_grad[None], f_grad)  38.8 us
    dot_general x16, matrix products, contract(): return jnp.einsum(form, left, right, preferred_element_type=jnp.float32)  26.3 us
    all_to_all x1, starting transfers between devices, per_device(): lax.all_to_all(query, 'seq', split_axis=1, concat_axis=0, tiled=True)  15.7 us
    all_to_all x1, waiting for transfers between devices, per_device(): lax.all_to_all(v_grad, 'seq', split_axis=0, concat_axis=1, tiled=True)  15.1 us
  transfers between devices with their start and end apart: 11, of which 5 were waited for; matrix products, arithmetic and copies ran while one was open for 23% of the time, Pallas kernels for 0%

profile of v1, /device:TPU:1, one launch (start us, length us, event | category | flops | bytes accessed | tf_op | source)
XLA Modules:
  0.0 656.4 jit_solution(2683780883471563055)
XLA Ops:
  9.4 15.7 %all-to-all-start = ((bf16[128,16,128]{0,2,1:T(8,128)(2,1)}), bf16[128,16,128]{0,2,1:T(8,128)(2,1)S(1)}, u32[]{:S(2)}, u32[]{:S(2)}) async-start(bf16[128,16,128]{0,2,1:T(8,128)(2,1)} %bitcast.18), calls=%async_computation | async-start | bytes 1048576 | tf_op jit(solution)/shard_map/all_to_all | solution.py:151
  31.7 46.4 %all_gather.3 = s32[1,2048]{1,0:T(1,128)S(1)} all-gather(s32[1,128]{1,0:T(1,128)S(1)} %copy-done.129), channel_id=1, replica_groups=mesh['dp'=32,'seq'=16] {'seq'}, dimensions={1}, use_global_device_ids=true | all-gather | bytes 8704 | tf_op jit(solution)/shard_map/all_gather | solution.py:142
  81.2 8.9 %all-to-all-start.1 = ((bf16[128,16,128]{0,2,1:T(8,128)(2,1)}), bf16[128,16,128]{0,2,1:T(8,128)(2,1)S(1)}, u32[]{:S(2)}, u32[]{:S(2)}) async-start(bf16[128,16,128]{0,2,1:T(8,128)(2,1)} %bitcast.21), calls=%async_computation.1 | async-start | bytes 1048576 | tf_op jit(solution)/shard_map/all_to_all | solution.py:152
  94.4 14.0 %all-to-all-done.1 = bf16[128,16,128]{0,2,1:T(8,128)(2,1)S(1)} async-done(((bf16[128,16,128]{0,2,1:T(8,128)(2,1)}), bf16[128,16,128]{0,2,1:T(8,128)(2,1)S(1)}, u32[]{:S(2)}, u32[]{:S(2)}) %all-to-all-start.1) | async-done | bytes 524320 | tf_op jit(solution)/shard_map/all_to_all | solution.py:152
  108.4 13.7 %all-to-all-start.2 = ((bf16[128,16,128]{0,2,1:T(8,128)(2,1)}), bf16[128,16,128]{0,2,1:T(8,128)(2,1)S(1)}, u32[]{:S(2)}, u32[]{:S(2)}) async-start(bf16[128,16,128]{0,2,1:T(8,128)(2,1)} %bitcast.24), calls=%async_computation.2 | async-start | bytes 1048576 | tf_op jit(solution)/shard_map/all_to_all | solution.py:154
  122.1 40.2 %fusion.322 = bf16[128,2048]{0,1:T(8,128)(2,1)S(1)} fusion(bf16[128,2048]{0,1:T(8,128)(2,1)S(1)} %bitcast.375, f32[2048]{0:T(1024)S(1)} %bitcast.429, f32[2048]{0:T(1024)S(1)} %bitcast.431, f32[2048]{0:T(1024)S(1)} %bitcast.435, f32[2048]{0:T(1024)S(1)} %bitcast.437, f32[2048]{0:T(1024)S(1)} %bitcast.439, f32[2048]{0:T(1024)S(1)} %bitcast.441, ...), kind=kLoop, calls=%fused_computation.710 | loop fusion | flops 116391936 | bytes 1838976 | tf_op jit(solution)/shard_map/convert_element_type | solution.py:149
  163.4 11.5 %all-to-all-start.3 = ((bf16[128,16,128]{2,0,1:T(8,128)(2,1)}), bf16[128,16,128]{2,0,1:T(8,128)(2,1)S(1)}, u32[]{:S(2)}, u32[]{:S(2)}) async-start(bf16[128,16,128]{2,0,1:T(8,128)(2,1)} %copy.195), calls=%async_computation.3 | async-start | bytes 1048576 | tf_op jit(solution)/shard_map/all_to_all | solution.py:153
  181.3 13.2 %all-to-all-done.3 = bf16[128,16,128]{2,0,1:T(8,128)(2,1)S(1)} async-done(((bf16[128,16,128]{2,0,1:T(8,128)(2,1)}), bf16[128,16,128]{2,0,1:T(8,128)(2,1)S(1)}, u32[]{:S(2)}, u32[]{:S(2)}) %all-to-all-start.3) | async-done | bytes 524320 | tf_op jit(solution)/shard_map/all_to_all | solution.py:153
  196.0 67.1 %while.18 = (s32[]{:T(128)}, bf16[2,2048,64]{1,2,0:T(8,128)(2,1)}, bf16[2,2048,64]{1,2,0:T(8,128)(2,1)}, bf16[2,2048,64]{1,2,0:T(8,128)(2,1)}, pred[16,4]{1,0:T(...) while((s32[]{:T(128)}, bf16[2,2048,64]{1,2,0:T(8,128)(2,1)}, ...), condition=%wide.region_6.7_spmd, body=%wide.region_1.6_spmd.sunk | while | flops 1074403328 | bytes 83230208 | solution.py:126
  198.6 4.9 fusion.503
  232.0 4.9 fusion.503
  265.6 14.2 %all-to-all-start.6 = ((bf16[16,128,128]{2,1,0:T(8,128)(2,1)}), bf16[16,128,128]{2,1,0:T(8,128)(2,1)S(1)}, u32[]{:S(2)}, u32[]{:S(2)}) async-start(bf16[16,128,128]{2,1,0:T(8,128)(2,1)} %copy.201), calls=%async_computation.6 | async-start | bytes 1048576 | tf_op jit(solution)/shard_map/all_to_all | solution.py:162
  286.2 15.1 %all-to-all-done.6 = bf16[16,128,128]{2,1,0:T(8,128)(2,1)S(1)} async-done(((bf16[16,128,128]{2,1,0:T(8,128)(2,1)}), bf16[16,128,128]{2,1,0:T(8,128)(2,1)S(1)}, u32[]{:S(2)}, u32[]{:S(2)}) %all-to-all-start.6) | async-done | bytes 524320 | tf_op jit(solution)/shard_map/all_to_all | solution.py:162
  301.3 12.9 %all-to-all-start.4 = ((bf16[16,128,128]{1,2,0:T(8,128)(2,1)}), bf16[16,128,128]{1,2,0:T(8,128)(2,1)S(1)}, u32[]{:S(2)}, u32[]{:S(2)}) async-start(bf16[16,128,128]{1,2,0:T(8,128)(2,1)} %copy.198), calls=%async_computation.4 | async-start | bytes 1048576 | tf_op jit(solution)/shard_map/all_to_all | solution.py:160
  322.0 4.2 fusion.247
  326.3 3.6 fusion.259
  337.2 4.0 fusion.295
  341.2 11.5 %all-to-all-start.5 = ((bf16[16,128,128]{2,1,0:T(8,128)(2,1)}), bf16[16,128,128]{2,1,0:T(8,128)(2,1)S(1)}, u32[]{:S(2)}, u32[]{:S(2)}) async-start(bf16[16,128,128]{2,1,0:T(8,128)(2,1)} %copy.199), calls=%async_computation.5 | async-start | bytes 1048576 | tf_op jit(solution)/shard_map/all_to_all | solution.py:161
  358.7 4.2 fusion.307
  362.9 4.2 fusion.319
  367.2 5.8 stack.259
  376.9 126.7 %all-reduce.3.cloned.1.call-done = f32[64,2048]{1,0:T(8,128)} async-done(((f32[64,2048]{1,0:T(8,128)}), f32[64,2048]{1,0:T(8,128)}) %all-reduce.3.cloned.1.call-update) | async-done | bytes 524304 | tf_op jit(solution)/shard_map/psum | solution.py:168
  504.0 38.8 %fusion.447 = bf16[1,128,2048]{1,2,0:T(8,128)(2,1)S(1)} fusion(f32[2048]{0:T(1024)S(1)} %bitcast.430, bf16[63,2048]{0,1:T(8,128)(2,1)S(1)} %collective-permute-done.1, bf16[128,2048]{0,1:T(8,128)(2,1)S(1)} %bitcast.391, pred[128]{0:T(512)(128)(4,1)} %get-tuple-element.460, f32[2048]{0:T(1024)S(1)} %bitcast.432, pred[128]{0:T(512)(128)(4,1)} %get-tuple-element.399, ...), kind=kLoop, calls=%fused_computation.838 | loop fusion | flops 116391936 | bytes 1838976 | tf_op jit(solution)/shard_map/broadcast_in_dim | solution.py:169
  543.8 103.7 %all-reduce.5.cloned.1.call-done = f32[64,2048]{1,0:T(8,128)} async-done(((f32[64,2048]{1,0:T(8,128)}), f32[64,2048]{1,0:T(8,128)}) %all-reduce.5.cloned.1.call-update) | async-done | bytes 524304 | tf_op jit(solution)/shard_map/psum | solution.py:168
  (407 shorter events, 116.9 us)
Async XLA Ops:
  9.4 71.8 %all-to-all-start = ((bf16[128,16,128]{0,2,1:T(8,128)(2,1)}), bf16[128,16,128]{0,2,1:T(8,128)(2,1)S(1)}, u32[]{:S(2)}, u32[]{:S(2)}) async-start(bf16[128,16,128]{0,2,1:T(8,128)(2,1)} %bitcast.18), calls=%async_computation | async-start | bytes 1048576 | tf_op jit(solution)/shard_map/all_to_all | solution.py:151
  27.4 94.7 %collective-permute-start = (bf16[63,2048]{0,1:T(8,128)(2,1)}, bf16[63,2048]{0,1:T(8,128)(2,1)S(1)}, u32[]{:S(2)}, u32[]{:S(2)}) collective-permute-start(bf16[63,2048]{0,1:T(8,128)(2,1)} %slice_bitcast_fusion), channel_id=1, source_target_pairs={{0,1},{1,2},{2,3},{3,4},{4,5},{5,6},{6,7},{7,8},{8,9},{9,10},{10,1... | collective-permute-start | bytes 774152 | tf_op jit(solution)/shard_map/ppermute | solution.py:13
  81.2 27.3 %all-to-all-start.1 = ((bf16[128,16,128]{0,2,1:T(8,128)(2,1)}), bf16[128,16,128]{0,2,1:T(8,128)(2,1)S(1)}, u32[]{:S(2)}, u32[]{:S(2)}) async-start(bf16[128,16,128]{0,2,1:T(8,128)(2,1)} %bitcast.21), calls=%async_computation.1 | async-start | bytes 1048576 | tf_op jit(solution)/shard_map/all_to_all | solution.py:152
  108.4 54.9 %all-to-all-start.2 = ((bf16[128,16,128]{0,2,1:T(8,128)(2,1)}), bf16[128,16,128]{0,2,1:T(8,128)(2,1)S(1)}, u32[]{:S(2)}, u32[]{:S(2)}) async-start(bf16[128,16,128]{0,2,1:T(8,128)(2,1)} %bitcast.24), calls=%async_computation.2 | async-start | bytes 1048576 | tf_op jit(solution)/shard_map/all_to_all | solution.py:154
  163.4 31.2 %all-to-all-start.3 = ((bf16[128,16,128]{2,0,1:T(8,128)(2,1)}), bf16[128,16,128]{2,0,1:T(8,128)(2,1)S(1)}, u32[]{:S(2)}, u32[]{:S(2)}) async-start(bf16[128,16,128]{2,0,1:T(8,128)(2,1)} %copy.195), calls=%async_computation.3 | async-start | bytes 1048576 | tf_op jit(solution)/shard_map/all_to_all | solution.py:153
  265.6 35.7 %all-to-all-start.6 = ((bf16[16,128,128]{2,1,0:T(8,128)(2,1)}), bf16[16,128,128]{2,1,0:T(8,128)(2,1)S(1)}, u32[]{:S(2)}, u32[]{:S(2)}) async-start(bf16[16,128,128]{2,1,0:T(8,128)(2,1)} %copy.201), calls=%async_computation.6 | async-start | bytes 1048576 | tf_op jit(solution)/shard_map/all_to_all | solution.py:162
  301.3 39.9 %all-to-all-start.4 = ((bf16[16,128,128]{1,2,0:T(8,128)(2,1)}), bf16[16,128,128]{1,2,0:T(8,128)(2,1)S(1)}, u32[]{:S(2)}, u32[]{:S(2)}) async-start(bf16[16,128,128]{1,2,0:T(8,128)(2,1)} %copy.198), calls=%async_computation.4 | async-start | bytes 1048576 | tf_op jit(solution)/shard_map/all_to_all | solution.py:160
  341.2 34.4 %all-to-all-start.5 = ((bf16[16,128,128]{2,1,0:T(8,128)(2,1)}), bf16[16,128,128]{2,1,0:T(8,128)(2,1)S(1)}, u32[]{:S(2)}, u32[]{:S(2)}) async-start(bf16[16,128,128]{2,1,0:T(8,128)(2,1)} %copy.199), calls=%async_computation.5 | async-start | bytes 1048576 | tf_op jit(solution)/shard_map/all_to_all | solution.py:161
  352.7 150.9 %all-reduce.3.cloned.1.call-start = ((), (), s32[]{:S(2)}) async-start(), calls=%async_computation.7 | async-start | bytes 1048576 | tf_op jit(solution)/shard_map/psum | solution.py:168
  358.3 145.3 %copy-start.10 = (f32[1,2048]{1,0:T(1,128)S(1)}, f32[1,2048]{1,0:T(1,128)}, u32[]{:S(2)}) copy-start(f32[1,2048]{1,0:T(1,128)} %copy-done.9) | copy-start | bytes 24580
  358.4 145.3 %copy-start.12 = (f32[1,2048]{1,0:T(1,128)S(1)}, f32[1,2048]{1,0:T(1,128)}, u32[]{:S(2)}) copy-start(f32[1,2048]{1,0:T(1,128)} %copy-done.11) | copy-start | bytes 24580
  358.4 145.3 %copy-start.14 = (f32[1,2048]{1,0:T(1,128)S(1)}, f32[1,2048]{1,0:T(1,128)}, u32[]{:S(2)}) copy-start(f32[1,2048]{1,0:T(1,128)} %copy-done.13) | copy-start | bytes 24580
  358.4 145.3 %copy-start.16 = (f32[1,2048]{1,0:T(1,128)S(1)}, f32[1,2048]{1,0:T(1,128)}, u32[]{:S(2)}) copy-start(f32[1,2048]{1,0:T(1,128)} %copy-done.15) | copy-start | bytes 24580
  358.4 145.3 %copy-start.18 = (f32[1,2048]{1,0:T(1,128)S(1)}, f32[1,2048]{1,0:T(1,128)}, u32[]{:S(2)}) copy-start(f32[1,2048]{1,0:T(1,128)} %copy-done.17) | copy-start | bytes 24580
  358.4 145.3 %copy-start.20 = (f32[1,2048]{1,0:T(1,128)S(1)}, f32[1,2048]{1,0:T(1,128)}, u32[]{:S(2)}) copy-start(f32[1,2048]{1,0:T(1,128)} %copy-done.19) | copy-start | bytes 24580
  358.4 145.3 %copy-start.22 = (f32[1,2048]{1,0:T(1,128)S(1)}, f32[1,2048]{1,0:T(1,128)}, u32[]{:S(2)}) copy-start(f32[1,2048]{1,0:T(1,128)} %copy-done.21) | copy-start | bytes 24580
  358.4 145.3 %copy-start.24 = (f32[1,2048]{1,0:T(1,128)S(1)}, f32[1,2048]{1,0:T(1,128)}, u32[]{:S(2)}) copy-start(f32[1,2048]{1,0:T(1,128)} %copy-done.23) | copy-start | bytes 24580
  358.4 145.3 %copy-start.26 = (f32[1,2048]{1,0:T(1,128)S(1)}, f32[1,2048]{1,0:T(1,128)}, u32[]{:S(2)}) copy-start(f32[1,2048]{1,0:T(1,128)} %copy-done.25) | copy-start | bytes 24580
  358.4 145.3 %copy-start.28 = (f32[1,2048]{1,0:T(1,128)S(1)}, f32[1,2048]{1,0:T(1,128)}, u32[]{:S(2)}) copy-start(f32[1,2048]{1,0:T(1,128)} %copy-done.27) | copy-start | bytes 24580
  358.4 145.3 %copy-start.30 = (f32[1,2048]{1,0:T(1,128)S(1)}, f32[1,2048]{1,0:T(1,128)}, u32[]{:S(2)}) copy-start(f32[1,2048]{1,0:T(1,128)} %copy-done.29) | copy-start | bytes 24580
  358.5 145.3 %copy-start.32 = (f32[1,2048]{1,0:T(1,128)S(1)}, f32[1,2048]{1,0:T(1,128)}, u32[]{:S(2)}) copy-start(f32[1,2048]{1,0:T(1,128)} %copy-done.31) | copy-start | bytes 24580
  358.5 145.3 %copy-start.34 = (f32[1,2048]{1,0:T(1,128)S(1)}, f32[1,2048]{1,0:T(1,128)}, u32[]{:S(2)}) copy-start(f32[1,2048]{1,0:T(1,128)} %copy-done.33) | copy-start | bytes 24580
  373.0 274.6 %all-reduce.5.cloned.1.call-start = ((), (), s32[]{:S(2)}) async-start(), calls=%async_computation.8 | async-start | bytes 1048576 | tf_op jit(solution)/shard_map/psum | solution.py:168
  373.1 130.5 %collective-permute-start.1 = (bf16[63,2048]{0,1:T(8,128)(2,1)S(1)}, bf16[63,2048]{0,1:T(8,128)(2,1)S(1)}, u32[]{:S(2)}, u32[]{:S(2)}) collective-permute-start(bf16[63,2048]{0,1:T(8,128)(2,1)S(1)} %bitcast.390), channel_id=1, source_target_pairs={{1,0},{2,1},{3,2},{4,3},{5,4},{6,5},{7,6},{8,7},{9,8},{10,9},{11,1... | collective-permute-start | bytes 774152 | tf_op jit(solution)/shard_map/ppermute | solution.py:13
  (121 other events, 8059.8 us)
Sparse Core Ops, SparseCore 0:
  373.1 130.4 all-reduce.2
  507.2 140.3 all-reduce.4
